TPU v7x, 32 devices: a whole 2x2x4 slice. The times are simulated.
32 devices in a mesh: dp: 4 (over z), feat: 8 (over y, x, core).
Axes of the slice: x: 2, y: 2, z: 4, core: 2. Of those that a mesh axis runs over, the one named last changes fastest.
Arguments:
- clip_feats: bfloat16 [2, 384, 8192], P(None, 'dp', 'feat'), may hold values from 0 to 60
- proj_weight: bfloat16 [8192, 8192], P('dp', 'feat'), may hold values from -0.0625 to 0.0625
Outputs:
- loss_value: float32 [], replicated
- weight_grad: float32 [8192, 8192], P('dp', 'feat')
- redundancy: float32 [], replicated
- pair_similarity: float32 [384, 384], P('dp')
All inputs are finite; a program needn't handle non-finite values.
Results may differ from a plain program's by a relative error of at most 0.034.
Values may be sent and summed in bfloat16 or wider, within the bound.
A program may use at most 64 MiB of HBM per device.

v0:
```python
import math
import jax
import jax.numpy as jnp
from jax import lax
from jax.sharding import PartitionSpec as P

D = 8192
off_weight = 0.0051
epsilon = 1e-05
grad_scale = 32.0


def per_device(clip_feats, proj_weight):
    pairs = clip_feats.shape[1]
    width = clip_feats.shape[2]
    depth = proj_weight.shape[0]
    dp_count = lax.axis_size("dp")
    total = pairs * dp_count
    pair_count = float(total)
    gathered = lax.all_gather(clip_feats, "feat", axis=0, tiled=False)
    rows = lax.all_to_all(gathered, "dp", split_axis=0, concat_axis=0, tiled=True)
    parts = depth // width
    rows = rows.reshape(dp_count, parts, 2 * pairs, width).transpose(1, 0, 2, 3)
    rows = rows.reshape(parts, 2 * total, width)
    partial = sum(
        (
            jnp.dot(
                rows[i],
                proj_weight[i * width : (i + 1) * width],
                preferred_element_type=jnp.float32,
            )
            for i in range(parts)
        )
    ).reshape(dp_count, 2, pairs, width)
    partial = partial - jnp.mean(partial, axis=(0, 2), keepdims=True)
    columns = width // dp_count
    pieces = partial.astype(jnp.bfloat16).reshape(2 * total, width)
    pieces = jnp.stack([pieces[:, i * columns : (i + 1) * columns] for i in range(dp_count)])
    pieces = lax.all_to_all(pieces, "dp", split_axis=0, concat_axis=0, tiled=True)
    centered = jnp.sum(pieces.astype(jnp.float32), axis=0)
    centered = (
        centered.reshape(dp_count, 2, pairs, columns)
        .transpose(1, 0, 2, 3)
        .reshape(2, total, columns)
    )
    col_var = jnp.mean(centered * centered, axis=1, keepdims=True)
    col_scale = lax.rsqrt(col_var + epsilon)
    normed = centered * col_scale
    quantized = normed.astype(jnp.bfloat16)
    widened = quantized.astype(jnp.float32)
    gram_part = jnp.einsum("vpc,vnc->vpn", quantized, quantized, preferred_element_type=jnp.float32)
    diag_corr = jnp.sum(widened[0] * widened[1], axis=0) / pair_count
    diag_part = jnp.sum((1.0 - diag_corr) ** 2 - off_weight * diag_corr * diag_corr)
    square_part = jnp.sum(diag_corr * diag_corr)
    grams, diag_term, squares = lax.psum((gram_part, diag_part, square_part), ("dp", "feat"))
    frob_scaled = jnp.sum(grams[0] * grams[1]) / (pair_count * pair_count)
    loss_value = 16.0 * (diag_term + off_weight * frob_scaled) / float(D)
    redundancy = 8.0 * pair_count * (frob_scaled - squares) / (float(D) * float(D))
    first_row = lax.axis_index("dp") * pairs
    own = lax.dynamic_slice_in_dim(grams, first_row, pairs, axis=1)
    row_ids = lax.broadcasted_iota(jnp.int32, (pairs, total), 0) + first_row
    col_ids = lax.broadcasted_iota(jnp.int32, (pairs, total), 1)
    pair_similarity = jnp.where(
        row_ids == col_ids, 0.0, (own[0] + own[1]) / (2.0 * math.sqrt(float(D)))
    )
    slope = -2.0 * (1.0 - diag_corr) - 2.0 * off_weight * diag_corr
    coefficient = 2.0 * off_weight / (pair_count * pair_count)
    gram_q = grams.astype(jnp.bfloat16)
    cross_first = jnp.dot(gram_q[1], quantized[0], preferred_element_type=jnp.float32)
    cross_second = jnp.dot(gram_q[0], quantized[1], preferred_element_type=jnp.float32)
    grad_norm = jnp.stack(
        [
            slope * widened[1] / pair_count + coefficient * cross_first,
            slope * widened[0] / pair_count + coefficient * cross_second,
        ]
    )
    mean_one = jnp.mean(grad_norm, axis=1, keepdims=True)
    mean_two = jnp.mean(grad_norm * normed, axis=1, keepdims=True)
    pre_q = (col_scale * (grad_norm - mean_one - normed * mean_two)).astype(jnp.bfloat16)
    pre_q = (
        pre_q.reshape(2, dp_count, pairs, columns).transpose(1, 0, 2, 3).reshape(2 * total, columns)
    )
    flat_grad = lax.all_gather(pre_q, "dp", axis=1, tiled=True)
    summed = jnp.concatenate(
        [jnp.dot(rows[i].T, flat_grad, preferred_element_type=jnp.float32) for i in range(parts)]
    )
    return (loss_value, grad_scale * summed, redundancy, pair_similarity)


def solution(mesh):
    placed = (P(None, "dp", "feat"), P("dp", "feat"))
    return jax.shard_map(
        per_device,
        mesh=mesh,
        in_specs=placed,
        out_specs=(P(), P("dp", "feat"), P(), P("dp", None)),
        check_vma=False,
    )
```

profile of v0, /device:TPU:12, one launch (start us, length us, event | category | flops | bytes accessed | tf_op | source)
XLA Modules:
  0.0 368.9 jit_solution(855138404987530139)
XLA Ops:
  7.2 0.0 all-gather.6.cloned.1.call-start
  7.2 0.7 all-gather.6.cloned.1.call-update
  7.9 0.0 all-reduce.3.cloned.1.call-start
  7.9 35.3 %all-gather.6.cloned.1.call-done = bf16[16,96,1024]{2,1,0:T(8,128)(2,1)} async-done(((bf16[2,96,1024]{2,1,0:T(8,128)(2,1)}), bf16[16,96,1024]{2,1,0:T(8,128)(2,1)}) %all-gather.6.cloned.1.call-update) | async-done | bytes 3145744 | tf_op jit(solution)/shard_map/all_gather | solution.py:20
  43.2 74.4 %all_to_all.10 = bf16[8,2,96,1024]{3,2,1,0:T(8,128)(2,1)S(1)} all-to-all(bf16[8,2,96,1024]{3,2,1,0:T(8,128)(2,1)} %bitcast.90), channel_id=1, replica_groups=mesh['dp'=4,'feat'=8] {'dp'}, dimensions={0} | all-to-all | bytes 6291456 | tf_op jit(solution)/shard_map/all_to_all | solution.py:21
  117.6 0.0 copy-start.5
  117.6 0.3 fusion.17
  117.9 0.0 copy-start.3
  117.9 0.0 copy-start.1
  118.0 3.0 copy-done.5
  120.9 1.8 fusion.1
  122.7 0.0 copy-done.3
  122.8 0.0 copy-done.1
  122.8 1.8 fusion.5
  124.6 0.2 reduce_sum.81
  124.8 0.4 fusion
  125.2 0.1 slice_bitcast_fusion.5
  125.3 0.2 pad_maximum_fusion
  125.6 39.1 %all_to_all.11 = bf16[4,768,256]{2,1,0:T(8,128)(2,1)S(1)} all-to-all(bf16[4,768,256]{2,1,0:T(8,128)(2,1)S(1)} %pad_maximum_fusion), channel_id=1, replica_groups=mesh['dp'=4,'feat'=8] {'dp'}, dimensions={0} | all-to-all | bytes 3145728 | tf_op jit(solution)/shard_map/all_to_all | solution.py:39
  164.7 0.2 convert_reduce_fusion
  164.9 0.1 multiply_reduce_fusion.1
  165.0 0.1 copy.9
  165.1 0.1 fusion.15
  165.2 1.4 fusion.18
  166.6 0.0 all-reduce.3.cloned.1.call-update
  166.6 0.0 all-gather.4.cloned.1.call-start
  166.7 0.1 multiply_reduce_fusion.2
  166.7 0.6 multiply_reduce_fusion.3
  167.3 129.9 %all-reduce.3.cloned.1.call-done = f32[2,384,384]{2,1,0:T(8,128)} async-done(((f32[2,384,384]{2,1,0:T(8,128)}), f32[2,384,384]{2,1,0:T(8,128)}) %all-reduce.3.cloned.1.call-update) | async-done | bytes 1179664 | tf_op jit(solution)/shard_map/psum | solution.py:55
  297.2 1.3 convert_element_type.24
  298.6 0.3 fusion.9
  298.8 0.3 fusion.8
  299.1 0.1 maximum_reduce_fusion
  299.2 0.1 multiply_reduce_fusion
  299.3 0.0 copy-start
  299.3 0.0 copy-start.4
  299.3 0.9 multiply_convert_fusion
  300.2 0.0 all-gather.4.cloned.1.call-update
  300.3 46.0 %all-reduce = (f32[]{:T(128)}, f32[]{:T(128)}) all-reduce(f32[]{:T(128)} %get-tuple-element.5, f32[]{:T(128)} %get-tuple-element.4), channel_id=1, replica_groups=mesh['dp'=4,'feat'=8] {'dp','feat'}, use_global_device_ids=true, to_apply=%region_5.0 | all-reduce | flops 2 | bytes 16 | tf_op jit(solution)/shard_map/psum | solution.py:55
  346.3 0.0 copy-done
  346.3 0.7 fusion.11
  349.7 0.7 fusion.14
  350.4 0.0 copy-start.2
  350.4 0.0 all-gather.4.cloned.1.call-done
  350.4 0.0 copy-done.4
  350.4 0.0 copy-start.6
  350.4 3.4 convolution_bitcast_fusion
  353.8 0.0 copy-done.2
  353.8 0.0 copy-done.6
  353.8 1.8 convolution_bitcast_fusion.1
  355.7 4.4 %maximum_multiply_fusion = f32[2048,1024]{1,0:T(8,128)} fusion(f32[1024,1024]{1,0:T(8,128)S(1)} %convolution_bitcast_fusion, f32[1024,1024]{1,0:T(8,128)S(1)} %convolution_bitcast_fusion.1), kind=kLoop, calls=%fused_computation | loop fusion | flops 4194304 | bytes 16777216 | tf_op jit(solution)/shard_map/mul | solution.py:87
  (4 shorter events, 0.0 us)
Async XLA Ops:
  7.2 36.1 %all-gather.6.cloned.1.call-start = ((), (), s32[]{:S(2)}) async-start(), calls=%async_computation.4 | async-start | bytes 3538944 | tf_op jit(solution)/shard_map/all_gather | solution.py:20
  7.9 289.3 %all-reduce.3.cloned.1.call-start = ((), (), s32[]{:S(2)}) async-start(), calls=%async_computation.2 | async-start | bytes 2359296 | tf_op jit(solution)/shard_map/psum | solution.py:55
  117.6 3.3 copy-start.5
  117.9 4.8 %copy-start.3 = (bf16[1,4,192,1024]{3,2,0,1:T(8,128)(2,1)}, bf16[1,4,192,1024]{3,2,0,1:T(8,128)(2,1)S(1)}, u32[]{:S(2)}) copy-start(bf16[1,4,192,1024]{3,2,0,1:T(8,128)(2,1)S(1)} %get-tuple-element.11) | copy-start | bytes 4718596
  117.9 4.8 %copy-start.1 = (bf16[1,4,192,1024]{3,2,0,1:T(8,128)(2,1)}, bf16[1,4,192,1024]{3,2,0,1:T(8,128)(2,1)S(1)}, u32[]{:S(2)}) copy-start(bf16[1,4,192,1024]{3,2,0,1:T(8,128)(2,1)S(1)} %get-tuple-element.10) | copy-start | bytes 4718596
  166.6 183.8 %all-gather.4.cloned.1.call-start = ((), (), s32[]{:S(2)}) async-start(), calls=%async_computation.3 | async-start | bytes 1966080 | tf_op jit(solution)/shard_map/all_gather | solution.py:83
  299.3 47.0 %copy-start = (f32[2,384,384]{2,1,0:T(8,128)S(1)}, f32[2,384,384]{2,1,0:T(8,128)}, u32[]{:S(2)}) copy-start(f32[2,384,384]{2,1,0:T(8,128)} %all-reduce.3.cloned.1.call-done) | copy-start | bytes 3538948
  299.3 51.1 %copy-start.4 = (bf16[1,4,192,1024]{3,2,0,1:T(8,128)(2,1)S(1)}, bf16[1,4,192,1024]{3,2,0,1:T(8,128)(2,1)}, u32[]{:S(2)}) copy-start(bf16[1,4,192,1024]{3,2,0,1:T(8,128)(2,1)} %copy-done.3) | copy-start | bytes 4718596
  350.4 3.4 copy-start.2
  350.4 3.4 copy-start.6
Sparse Core Ops, SparseCore 0:
  9.9 33.3 all-gather.5
  166.7 130.4 all-reduce.2
  300.4 35.5 all-gather.3
where the time goes:
time: 369 us
  waiting for transfers between devices  166 us (45%)
  blocking collectives  160 us (43%)
  between operations  18.8 us (5%)
  matrix products  10.8 us (3%)
  other arithmetic  10.2 us (3%)
    psum x1, waiting for transfers between devices, per_device(): lax.psum((gram_part, diag_part, square_part), ('dp', 'feat'))  130 us
    all_to_all x1, blocking collectives, per_device(): lax.all_to_all(gathered, 'dp', split_axis=0, concat_axis=0, tiled=True)  74.4 us
    psum x1, blocking collectives, per_device(): lax.psum((gram_part, diag_part, square_part), ('dp', 'feat'))  46 us
    all_to_all x1, blocking collectives, per_device(): lax.all_to_all(pieces, 'dp', split_axis=0, concat_axis=0, tiled=True)  39.1 us
    all_gather x1, waiting for transfers between devices, per_device(): gathered = lax.all_gather(clip_feats, 'feat', axis=0, tiled=False)  35.3 us
  transfers between devices with their start and end apart: 3, of which 2 were waited for; matrix products, arithmetic and copies ran while one was open for 1% of the time, Pallas kernels for 0%

commit v1 on v0

--- a/solution.py
+++ b/solution.py
@@ -52,7 +52,9 @@
     diag_corr = jnp.sum(widened[0] * widened[1], axis=0) / pair_count
     diag_part = jnp.sum((1.0 - diag_corr) ** 2 - off_weight * diag_corr * diag_corr)
     square_part = jnp.sum(diag_corr * diag_corr)
-    grams, diag_term, squares = lax.psum((gram_part, diag_part, square_part), ("dp", "feat"))
+    grams, diag_term, squares = lax.psum(
+        lax.psum((gram_part, diag_part, square_part), "feat"), "dp"
+    )
     frob_scaled = jnp.sum(grams[0] * grams[1]) / (pair_count * pair_count)
     loss_value = 16.0 * (diag_term + off_weight * frob_scaled) / float(D)
     redundancy = 8.0 * pair_count * (frob_scaled - squares) / (float(D) * float(D))

time: 369 us -> 342 us (0.927); the launches traced: 369 us -> 338 us
  blocking collectives: 160 us -> 137 us
  waiting for transfers between devices: 166 us -> 158 us
    psum x1 -> x2, blocking collectives: 46 us -> 23.2 us  [the longest x1 13.1 us: per_device(): lax.psum((gram_part, diag_part, square_part), 'feat')]
    psum x1 -> x2, waiting for transfers between devices: 130 us -> 113 us  [the longest x1 57.6 us: per_device(): lax.psum(lax.psum((gram_part, diag_part, square_part), 'feat'), 'dp')]
    all_gather x1, waiting for transfers between devices: 0.01 us -> 8.25 us  [per_device(): flat_grad = lax.all_gather(pre_q, 'dp', axis=1, tiled=True)]
  transfers between devices with their start and end apart: 3 -> 4, of which waited for: 2 -> 4; matrix products, arithmetic and copies ran while one was open for 1% -> 1% of each run, Pallas kernels for 0% -> 0%
where the time goes in v1:
time: 342 us; the launch traced here: 338 us
  waiting for transfers between devices  158 us (46%)
  blocking collectives  137 us (40%)
  between operations  18.8 us (5%)
  matrix products  10.8 us (3%)
  other arithmetic  10.2 us (3%)
  local copies, waits for them, and re-layouts  3.5 us (1%)
    all_to_all x1, blocking collectives, per_device(): lax.all_to_all(gathered, 'dp', split_axis=0, concat_axis=0, tiled=True)  74.4 us
    psum x1, waiting for transfers between devices, per_device(): lax.psum(lax.psum((gram_part, diag_part, square_part), 'feat'), 'dp')  57.6 us
    psum x1, waiting for transfers between devices, per_device(): lax.psum((gram_part, diag_part, square_part), 'feat')  55.8 us
    all_to_all x1, blocking collectives, per_device(): lax.all_to_all(pieces, 'dp', split_axis=0, concat_axis=0, tiled=True)  39.1 us
    all_gather x1, waiting for transfers between devices, per_device(): gathered = lax.all_gather(clip_feats, 'feat', axis=0, tiled=False)  35.3 us
    psum x1, blocking collectives, per_device(): lax.psum((gram_part, diag_part, square_part), 'feat')  13.1 us
    psum x1, blocking collectives, per_device(): lax.psum(lax.psum((gram_part, diag_part, square_part), 'feat'), 'dp')  10.1 us
    all_gather x1, waiting for transfers between devices, per_device(): flat_grad = lax.all_gather(pre_q, 'dp', axis=1, tiled=True)  8.25 us
  transfers between devices with their start and end apart: 4, of which 4 were waited for; matrix products, arithmetic and copies ran while one was open for 1% of the time, Pallas kernels for 0%

profile of v1, /device:TPU:12, one launch (start us, length us, event | category | flops | bytes accessed | tf_op | source)
XLA Modules:
  0.0 338.0 jit_solution(8771795915944411042)
XLA Ops:
  7.2 0.0 all-gather.6.cloned.1.call-start
  7.2 0.7 all-gather.6.cloned.1.call-update
  7.9 0.0 all-reduce.5.cloned.1.call-start
  7.9 35.3 %all-gather.6.cloned.1.call-done = bf16[16,96,1024]{2,1,0:T(8,128)(2,1)} async-done(((bf16[2,96,1024]{2,1,0:T(8,128)(2,1)}), bf16[16,96,1024]{2,1,0:T(8,128)(2,1)}) %all-gather.6.cloned.1.call-update) | async-done | bytes 3145744 | tf_op jit(solution)/shard_map/all_gather | solution.py:20
  43.2 74.4 %all_to_all.10 = bf16[8,2,96,1024]{3,2,1,0:T(8,128)(2,1)S(1)} all-to-all(bf16[8,2,96,1024]{3,2,1,0:T(8,128)(2,1)} %bitcast.90), channel_id=1, replica_groups=mesh['dp'=4,'feat'=8] {'dp'}, dimensions={0} | all-to-all | bytes 6291456 | tf_op jit(solution)/shard_map/all_to_all | solution.py:21
  117.6 0.0 copy-start.5
  117.6 0.3 fusion.17
  117.9 0.0 copy-start.3
  117.9 0.0 copy-start.1
  118.0 3.0 copy-done.5
  120.9 1.8 fusion.1
  122.7 0.0 copy-done.3
  122.8 0.0 copy-done.1
  122.8 1.8 fusion.5
  124.6 0.2 reduce_sum.81
  124.8 0.4 fusion
  125.2 0.1 slice_bitcast_fusion.5
  125.3 0.2 pad_maximum_fusion
  125.6 39.1 %all_to_all.11 = bf16[4,768,256]{2,1,0:T(8,128)(2,1)S(1)} all-to-all(bf16[4,768,256]{2,1,0:T(8,128)(2,1)S(1)} %pad_maximum_fusion), channel_id=1, replica_groups=mesh['dp'=4,'feat'=8] {'dp'}, dimensions={0} | all-to-all | bytes 3145728 | tf_op jit(solution)/shard_map/all_to_all | solution.py:39
  164.7 0.2 convert_reduce_fusion
  164.9 0.1 multiply_reduce_fusion.1
  165.0 0.1 copy.9
  165.1 0.1 fusion.15
  165.2 1.4 fusion.18
  166.6 0.0 all-reduce.5.cloned.1.call-update
  166.6 0.0 all-reduce.7.cloned.1.call-start
  166.7 55.8 %all-reduce.5.cloned.1.call-done = f32[2,384,384]{2,1,0:T(8,128)} async-done(((f32[2,384,384]{2,1,0:T(8,128)}), f32[2,384,384]{2,1,0:T(8,128)}) %all-reduce.5.cloned.1.call-update) | async-done | bytes 1179664 | tf_op jit(solution)/shard_map/psum | solution.py:56
  222.5 0.0 all-reduce.7.cloned.1.call-update
  222.5 0.0 all-gather.4.cloned.1.call-start
  222.6 0.1 multiply_reduce_fusion.2
  222.7 0.6 multiply_reduce_fusion.3
  223.3 57.6 %all-reduce.7.cloned.1.call-done = f32[2,384,384]{2,1,0:T(8,128)} async-done(((f32[2,384,384]{2,1,0:T(8,128)}), f32[2,384,384]{2,1,0:T(8,128)}) %all-reduce.7.cloned.1.call-update) | async-done | bytes 1179664 | tf_op jit(solution)/shard_map/psum | solution.py:55
  280.9 1.3 convert_element_type.24
  282.2 0.3 fusion.9
  282.5 0.3 fusion.8
  282.8 0.1 maximum_reduce_fusion
  282.9 0.1 multiply_reduce_fusion
  283.0 0.0 copy-start
  283.0 0.0 copy-start.4
  283.0 0.9 multiply_convert_fusion
  283.9 0.0 all-gather.4.cloned.1.call-update
  284.0 13.1 %all-reduce = (f32[]{:T(128)}, f32[]{:T(128)}) all-reduce(f32[]{:T(128)} %get-tuple-element.5, f32[]{:T(128)} %get-tuple-element.4), channel_id=1, replica_groups=mesh['dp'=4,'feat'=8] {'feat'}, use_global_device_ids=true, to_apply=%region_5.0 | all-reduce | flops 2 | bytes 16 | tf_op jit(solution)/shard_map/psum | solution.py:56
  297.1 10.1 %all-reduce.1 = (f32[]{:T(128)}, f32[]{:T(128)}) all-reduce(f32[]{:T(128)} %get-tuple-element.6, f32[]{:T(128)} %get-tuple-element.7), channel_id=1, replica_groups=mesh['dp'=4,'feat'=8] {'dp'}, use_global_device_ids=true, to_apply=%region_6.0 | all-reduce | flops 2 | bytes 16 | tf_op jit(solution)/shard_map/psum | solution.py:55
  307.2 0.0 copy-done
  307.2 0.7 fusion.11
  310.5 0.7 fusion.14
  311.3 0.0 copy-start.2
  311.3 8.3 %all-gather.4.cloned.1.call-done = bf16[768,1024]{1,0:T(8,128)(2,1)} async-done(((bf16[768,256]{1,0:T(8,128)(2,1)}), bf16[768,1024]{1,0:T(8,128)(2,1)}) %all-gather.4.cloned.1.call-update) | async-done | bytes 1572880 | tf_op jit(solution)/shard_map/all_gather | solution.py:85
  319.5 0.0 copy-done.4
  319.6 0.0 copy-start.6
  319.6 3.4 %convolution_bitcast_fusion = f32[1024,1024]{1,0:T(8,128)S(1)} fusion(bf16[768,1024]{1,0:T(8,128)(2,1)} %all-gather.4.cloned.1.call-done, bf16[768,1024]{1,0:T(8,128)(2,1)S(1)} %bitcast.95), kind=kOutput, calls=%fused_computation.4 | convolution fusion | flops 1610612736 | bytes 7340032 | tf_op jit(solution)/shard_map/dot_general | solution.py:87
  323.0 0.0 copy-done.2
  323.0 0.0 copy-done.6
  323.0 1.8 convolution_bitcast_fusion.1
  324.8 4.4 %maximum_multiply_fusion = f32[2048,1024]{1,0:T(8,128)} fusion(f32[1024,1024]{1,0:T(8,128)S(1)} %convolution_bitcast_fusion, f32[1024,1024]{1,0:T(8,128)S(1)} %convolution_bitcast_fusion.1), kind=kLoop, calls=%fused_computation | loop fusion | flops 4194304 | bytes 16777216 | tf_op jit(solution)/shard_map/mul | solution.py:89
  (4 shorter events, 0.0 us)
Async XLA Ops:
  7.2 36.1 %all-gather.6.cloned.1.call-start = ((), (), s32[]{:S(2)}) async-start(), calls=%async_computation.5 | async-start | bytes 3538944 | tf_op jit(solution)/shard_map/all_gather | solution.py:20
  7.9 214.6 %all-reduce.5.cloned.1.call-start = ((), (), s32[]{:S(2)}) async-start(), calls=%async_computation.2 | async-start | bytes 2359296 | tf_op jit(solution)/shard_map/psum | solution.py:56
  117.6 3.3 copy-start.5
  117.9 4.8 %copy-start.3 = (bf16[1,4,192,1024]{3,2,0,1:T(8,128)(2,1)}, bf16[1,4,192,1024]{3,2,0,1:T(8,128)(2,1)S(1)}, u32[]{:S(2)}) copy-start(bf16[1,4,192,1024]{3,2,0,1:T(8,128)(2,1)S(1)} %get-tuple-element.13) | copy-start | bytes 4718596
  117.9 4.8 %copy-start.1 = (bf16[1,4,192,1024]{3,2,0,1:T(8,128)(2,1)}, bf16[1,4,192,1024]{3,2,0,1:T(8,128)(2,1)S(1)}, u32[]{:S(2)}) copy-start(bf16[1,4,192,1024]{3,2,0,1:T(8,128)(2,1)S(1)} %get-tuple-element.12) | copy-start | bytes 4718596
  166.6 114.3 %all-reduce.7.cloned.1.call-start = ((), (), s32[]{:S(2)}) async-start(), calls=%async_computation.3 | async-start | bytes 2359296 | tf_op jit(solution)/shard_map/psum | solution.py:55
  222.5 97.0 %all-gather.4.cloned.1.call-start = ((), (), s32[]{:S(2)}) async-start(), calls=%async_computation.4 | async-start | bytes 1966080 | tf_op jit(solution)/shard_map/all_gather | solution.py:85
  283.0 24.2 %copy-start = (f32[2,384,384]{2,1,0:T(8,128)S(1)}, f32[2,384,384]{2,1,0:T(8,128)}, u32[]{:S(2)}) copy-start(f32[2,384,384]{2,1,0:T(8,128)} %all-reduce.7.cloned.1.call-done) | copy-start | bytes 3538948
  283.0 36.6 %copy-start.4 = (bf16[1,4,192,1024]{3,2,0,1:T(8,128)(2,1)S(1)}, bf16[1,4,192,1024]{3,2,0,1:T(8,128)(2,1)}, u32[]{:S(2)}) copy-start(bf16[1,4,192,1024]{3,2,0,1:T(8,128)(2,1)} %copy-done.3) | copy-start | bytes 4718596
  311.3 11.7 %copy-start.2 = (bf16[1,4,192,1024]{3,2,0,1:T(8,128)(2,1)S(1)}, bf16[1,4,192,1024]{3,2,0,1:T(8,128)(2,1)}, u32[]{:S(2)}) copy-start(bf16[1,4,192,1024]{3,2,0,1:T(8,128)(2,1)} %copy-done.1) | copy-start | bytes 4718596
  319.6 3.4 %copy-start.6 = (bf16[768,1024]{1,0:T(8,128)(2,1)S(1)}, bf16[768,1024]{1,0:T(8,128)(2,1)}, u32[]{:S(2)}) copy-start(bf16[768,1024]{1,0:T(8,128)(2,1)} %all-gather.4.cloned.1.call-done) | copy-start | bytes 4718596
Sparse Core Ops, SparseCore 0:
  9.9 33.3 all-gather.5
  166.7 55.7 all-reduce.4
  225.0 55.8 all-reduce.6
  284.1 35.4 all-gather.3
